TPU v7x, 256 devices: a whole 4x4x8 slice. The times are simulated.
256 devices in a mesh: dp: 32 (over y, z), vocab: 8 (over x, core).
Axes of the slice: x: 4, y: 4, z: 8, core: 2. Of those that a mesh axis runs over, the one named last changes fastest.
Arguments:
- draft_logits: bfloat16 [4096, 128000], P('dp', 'vocab'), may hold values from -15 to 250
- hidden: bfloat16 [4096, 2304], P('dp'), may hold values from -40 to 40
- embed_cot: bfloat16 [4096, 2304], P('dp'), may hold values from -0.59765625 to 0.59765625
- draft_ids: int32 [4096], P('dp'), may hold values from 0 to 127999, as said below
- target_ids: int32 [4096, 32], P('dp'), may hold values from 0 to 128255
- target_logits: float32 [4096, 32], P('dp'), may hold values from -8 to 240
- vocab_map: int32 [128256], replicated, may hold values from 0 to 127999
- master: float32 [128000, 2304], P(('vocab', 'dp')), may hold values from -6 to 6
- row_moment: float32 [128000], P(('vocab', 'dp')), may hold values from 0.0001 to 0.5
- col_moment: float32 [2304], replicated, may hold values from 0.003 to 0.03
Outputs:
- direction: bfloat16 [128000, 2304], P(('vocab', 'dp'))
- row_new: float32 [128000], P(('vocab', 'dp'))
- col_new: float32 [2304], replicated
- next_rows: bfloat16 [4096, 2304], P('dp')
Inputs may be any that keep to these rules, and one draw needn't show every extreme that they name: `draft_ids`: among the 128 tokens of one index of dp, at most 20 have draft ids in any one block of 16000 consecutive ids, and some block holds exactly 20 of them.
All inputs are finite; a program needn't handle non-finite values.
Results may differ from a plain program's by a relative error of at most 0.0073.
Values may be sent and summed in bfloat16 or wider, within the bound.
No kernel may reach another device: no remote copies, remote signals or barrier semaphores. Data moves between devices by JAX's collectives and lax.ppermute only.
A program may use at most 128 MiB of HBM per device.

v0:
```python
import jax
import jax.numpy as jnp
from jax import lax
from jax.sharding import PartitionSpec as P

DECAY_RATE = 0.9
STEP_SCALE = 0.01
SQUARE_EPS = 1e-30


def body(
    draft_logits,
    hidden,
    embed_cot,
    draft_ids,
    target_ids,
    target_logits,
    vocab_map,
    master,
    row_moment,
    col_moment,
):
    tokens_here, shard_cols = draft_logits.shape
    owned_rows, features = master.shape
    dp_count = lax.axis_size("dp")
    vocab_count = lax.axis_size("vocab")
    vocab_index = lax.axis_index("vocab")
    dp_index = lax.axis_index("dp")
    logits = draft_logits.astype(jnp.float32)
    local_max = jnp.max(logits, axis=1)
    highest = lax.pmax(local_max, "vocab")
    totals = lax.psum(jnp.sum(jnp.exp(logits - highest[:, None]), axis=1), "vocab")
    probs = jnp.exp(logits - highest[:, None]) / totals[:, None]
    shifted = target_logits - jnp.max(target_logits, axis=1, keepdims=True)
    target_exp = jnp.exp(shifted)
    weights = target_exp / jnp.sum(target_exp, axis=1, keepdims=True)
    mapped = vocab_map[target_ids] - vocab_index * shard_cols
    inside = (mapped >= 0) & (mapped < shard_cols)
    token_index = jnp.broadcast_to(
        jnp.arange(tokens_here, dtype=jnp.int32)[:, None], target_ids.shape
    )
    target = (
        jnp.zeros((tokens_here, shard_cols), jnp.float32)
        .at[token_index, jnp.clip(mapped, 0, shard_cols - 1)]
        .add(jnp.where(inside, weights, jnp.zeros_like(weights)))
    )
    slopes = (probs - target).astype(jnp.bfloat16)
    owned_slopes = lax.all_to_all(slopes, "dp", split_axis=1, concat_axis=0, tiled=True)
    head_grad = jnp.einsum(
        "tv,td->vd",
        owned_slopes,
        lax.all_gather(hidden, "dp", axis=0, tiled=True),
        preferred_element_type=jnp.float32,
    )
    block_base = vocab_index * shard_cols
    in_shard = (draft_ids >= block_base) & (draft_ids < block_base + shard_cols)
    slot_count = tokens_here // vocab_count + tokens_here // (4 * vocab_count)
    position = jnp.cumsum(in_shard.astype(jnp.int32)) - 1
    placing = (position[None, :] == jnp.arange(slot_count, dtype=jnp.int32)[:, None]) & in_shard[
        None, :
    ]
    filled = jnp.any(placing, axis=1)
    packed_ids = jnp.where(filled, jnp.sum(jnp.where(placing, draft_ids[None, :], 0), axis=1), -1)
    placing_half = placing.astype(jnp.bfloat16)
    packed_cot = jnp.dot(placing_half, embed_cot, preferred_element_type=jnp.float32).astype(
        jnp.bfloat16
    )
    all_ids, all_cot = (
        lax.all_gather(packed_ids, "dp", axis=0, tiled=True),
        lax.all_gather(packed_cot, "dp", axis=0, tiled=True),
    )
    row_base = (vocab_index * dp_count + dp_index) * owned_rows
    row_iota = jnp.arange(owned_rows, dtype=jnp.int32)
    matches = (all_ids[None, :] - row_base == row_iota[:, None]).astype(jnp.bfloat16)
    grad = head_grad + jnp.dot(matches, all_cot, preferred_element_type=jnp.float32)
    squares = grad * grad + SQUARE_EPS
    row_new = DECAY_RATE * row_moment + (1.0 - DECAY_RATE) * jnp.mean(squares, axis=1)
    column_total, row_total = lax.psum(
        (jnp.sum(squares, axis=0), jnp.sum(row_new)), ("dp", "vocab")
    )
    vocab_rows = owned_rows * dp_count * vocab_count
    col_new = DECAY_RATE * col_moment + (1.0 - DECAY_RATE) * (column_total / vocab_rows)
    scale = row_new[:, None] * col_new[None, :] / (row_total / vocab_rows)
    direction = grad / jnp.sqrt(scale)
    fresh = (master - STEP_SCALE * direction).astype(jnp.bfloat16)
    wanted = all_ids - row_base
    select = (wanted[:, None] == row_iota[None, :]).astype(jnp.bfloat16)
    slot_values = lax.psum_scatter(
        jnp.dot(select, fresh, preferred_element_type=jnp.float32).astype(jnp.bfloat16),
        "dp",
        scatter_dimension=0,
        tiled=True,
    )
    spread = jnp.einsum("st,sd->td", placing_half, slot_values, preferred_element_type=jnp.float32)
    next_rows = lax.psum(spread.astype(jnp.bfloat16), "vocab")
    return (direction.astype(jnp.bfloat16), row_new, col_new, next_rows)


def solution(mesh):
    in_specs = (
        P("dp", "vocab"),
        P("dp", None),
        P("dp", None),
        P("dp"),
        P("dp", None),
        P("dp", None),
        P(),
        P(("vocab", "dp"), None),
        P(("vocab", "dp")),
        P(),
    )
    out_specs = (P(("vocab", "dp"), None), P(("vocab", "dp")), P(), P("dp", None))
    return jax.shard_map(body, mesh=mesh, in_specs=in_specs, out_specs=out_specs, check_vma=False)
```

profile of v0, /device:TPU:8, one launch (start us, length us, event | category | flops | bytes accessed | tf_op | source)
XLA Modules:
  0.0 619.0 jit_solution(5468428876925927025)
XLA Ops:
  11.0 23.0 %gather_fusion = s32[4096]{0:T(1024)S(1)} fusion(s32[128256]{0:T(1024)S(1)} %copy-done.2, s32[4096]{0:T(1024)S(1)} %broadcast_clamp_fusion), kind=kCustom, calls=%fused_computation | custom fusion | bytes 49152 | tf_op jit(solution)/shard_map/gather | solution.py:37
  35.2 31.6 %scatter_custom_fusion = f32[2048000]{0:T(1024)} fusion(s32[4096]{0:T(1024)S(1)} %reshape.100, f32[4096]{0:T(1024)S(1)} %reshape.102, f32[]{:T(128)} %constant.21.clone.1), kind=kCustom, calls=%fused_computation.10 | custom fusion | flops 4096 | bytes 8192004
  66.8 9.1 %reshape.90 = f32[128,16000]{1,0:T(8,128)} reshape(f32[2048000]{0:T(1024)} %scatter_custom_fusion) | data formatting | bytes 16384000 | tf_op jit(solution)/shard_map/scatter-add | solution.py:45
  75.9 2.9 reduce_max.23
  78.8 13.1 %pmax.7 = f32[128]{0:T(128)S(1)} all-reduce(bf16[128]{0:T(256)(128)(2,1)S(1)} %reduce_max.23), channel_id=1, replica_groups=mesh['dp'=32,'vocab'=8] {'vocab'}, use_global_device_ids=true, to_apply=%region_1.0 | all-reduce | flops 128 | bytes 768 | tf_op jit(solution)/shard_map/pmax | solution.py:31
  91.9 3.7 fusion.1
  95.5 12.4 %psum.28 = f32[128]{0:T(128)S(1)} all-reduce(f32[128]{0:T(128)S(1)} %fusion.1), channel_id=1, replica_groups=mesh['dp'=32,'vocab'=8] {'vocab'}, use_global_device_ids=true, to_apply=%region_3.0 | all-reduce | flops 128 | bytes 1024 | tf_op jit(solution)/shard_map/psum | solution.py:32
  108.0 6.9 %subtract_convert_fusion = bf16[128,16000]{1,0:T(8,128)(2,1)} fusion(f32[128,16000]{1,0:T(8,128)} %reshape.90, bf16[128,16000]{1,0:T(8,128)(2,1)} %param.10, f32[128]{0:T(128)S(1)} %psum.28, f32[128]{0:T(128)S(1)} %pmax.7), kind=kLoop, calls=%fused_computation.2 | loop fusion | flops 10240000 | bytes 16385024 | tf_op jit(solution)/shard_map/convert_element_type | solution.py:47
  114.9 10.9 %reshape.126 = bf16[128,32,500]{2,1,0:T(8,128)(2,1)} reshape(bf16[128,16000]{1,0:T(8,128)(2,1)} %subtract_convert_fusion) | data formatting | bytes 8192000 | tf_op jit(solution)/shard_map/all_to_all | solution.py:48
  125.7 7.9 %copy.40 = bf16[128,32,500]{0,2,1:T(8,128)(2,1)} copy(bf16[128,32,500]{2,1,0:T(8,128)(2,1)} %reshape.126) | data formatting | bytes 8192000 | tf_op jit(solution)/shard_map/all_to_all | solution.py:48
  133.6 11.5 %all-to-all-start = ((bf16[128,32,500]{0,2,1:T(8,128)(2,1)}), bf16[128,32,500]{0,2,1:T(8,128)(2,1)}, u32[]{:S(2)}, u32[]{:S(2)}) async-start(bf16[128,32,500]{0,2,1:T(8,128)(2,1)} %copy.40), calls=%async_computation | async-start | bytes 8257536 | tf_op jit(solution)/shard_map/all_to_all | solution.py:48
  146.8 146.2 %all-reduce = s32[640]{0:T(1024)S(1)} all-reduce(s32[640]{0:T(1024)S(1)} %select_dynamic-update-slice_fusion), channel_id=1, replica_groups=mesh['dp'=32,'vocab'=8] {'dp'}, use_global_device_ids=true, to_apply=%add | all-reduce | flops 640 | bytes 5120
  293.0 3.8 reshape.123
  296.8 4.1 fusion.8
  301.0 6.6 %copy.38 = bf16[32,128,500]{2,1,0:T(8,128)(2,1)} copy(bf16[32,128,500]{1,2,0:T(8,128)(2,1)} %bitcast) | data formatting | bytes 8192000 | tf_op jit(solution)/shard_map/all_to_all | solution.py:48
  307.5 18.4 %all-gather.4.cloned.1.call-done = bf16[4096,2304]{1,0:T(8,128)(2,1)} async-done(((bf16[128,2304]{1,0:T(8,128)(2,1)}), bf16[4096,2304]{1,0:T(8,128)(2,1)}) %all-gather.4.cloned.1.call-update) | async-done | bytes 18874384 | tf_op jit(solution)/shard_map/all_gather | solution.py:52
  326.0 18.5 %fusion.4 = (f32[2304]{0:T(1024)S(1)}, f32[500]{0:T(512)S(1)}, f32[500,2304]{1,0:T(8,128)}) fusion(f32[500,2304]{1,0:T(8,128)} %fusion.8, bf16[4096,500]{1,0:T(8,128)(2,1)} %bitcast.14, bf16[4096,2304]{1,0:T(8,128)(2,1)} %all-gather.4.cloned.1.call-done), kind=kOutput, calls=%fused_computation.12 | convolution fusion | flops 9442941952 | bytes 32197584 | tf_op jit(solution)/shard_map/tv,td->vd/dot_general | solution.py:49
  345.1 74.8 %all-reduce.3 = (f32[]{:T(128)}, f32[2304]{0:T(1024)S(1)}) all-reduce(f32[]{:T(128)} %get-tuple-element.8, f32[2304]{0:T(1024)S(1)} %get-tuple-element.4), channel_id=1, replica_groups=mesh['dp'=32,'vocab'=8] {'dp','vocab'}, use_global_device_ids=true, to_apply=%region_14.15 | all-reduce | flops 2305 | bytes 18440 | tf_op jit(solution)/shard_map/psum | solution.py:78
  420.6 5.8 convolution_convert_fusion
  426.4 79.6 %fusion = bf16[24,2304]{1,0:T(8,128)(2,1)S(1)} fusion(bf16[640,2304]{1,0:T(8,128)(2,1)S(1)} %convolution_convert_fusion), kind=kCustom, calls=%all-reduce-scatter | all-reduce-scatter fusion | flops 1769473 | bytes 3060736
  506.1 1.9 collective-permute-start.5
  508.0 2.1 collective-permute-start
  510.2 4.7 collective-permute-start.1
  514.9 3.3 collective-permute-start.2
  518.1 7.8 %collective-permute-start.3 = (bf16[24,2304]{1,0:T(8,128)(2,1)S(1)}, bf16[24,2304]{1,0:T(8,128)(2,1)S(1)}, u32[]{:S(2)}, u32[]{:S(2)}) collective-permute-start(bf16[24,2304]{1,0:T(8,128)(2,1)S(1)} %fusion), channel_id=1, source_target_pairs={{0,32},{8,40},{16,48},{24,56},{32,64},{40,72},{48,80},{56,88},{64,... | collective-permute-start | bytes 331784
  526.0 8.8 %collective-permute-start.4 = (bf16[24,2304]{1,0:T(8,128)(2,1)S(1)}, bf16[24,2304]{1,0:T(8,128)(2,1)S(1)}, u32[]{:S(2)}, u32[]{:S(2)}) collective-permute-start(bf16[24,2304]{1,0:T(8,128)(2,1)S(1)} %fusion), channel_id=1, source_target_pairs={{0,40},{8,48},{16,56},{24,64},{32,72},{40,80},{48,88},{56,96},{64,... | collective-permute-start | bytes 331784
  535.5 1.6 collective-permute-done.4
  537.1 2.1 concatenate.4
  539.2 1.9 convolution_convert_fusion.1
  541.1 4.5 fusion.23
  545.6 64.9 %all-reduce.6.cloned.1.call-done = bf16[128,2304]{1,0:T(8,128)(2,1)} async-done(((bf16[128,2304]{1,0:T(8,128)(2,1)}), bf16[128,2304]{1,0:T(8,128)(2,1)}) %all-reduce.6.cloned.1.call-update) | async-done | bytes 589840 | tf_op jit(solution)/shard_map/psum | solution.py:95
  610.5 1.9 copy.43
  (78 shorter events, 6.6 us)
Async XLA Ops:
  7.2 1.2 copy-start
  7.2 3.8 copy-start.2
  7.2 285.8 %all-gather.6.cloned.1.call-start = ((), (), s32[]{:S(2)}) async-start(), calls=%async_computation.3 | async-start | bytes 3649536 | tf_op jit(solution)/shard_map/all_gather | solution.py:70
  8.0 138.6 %copy-start.9 = (pred[128]{0:T(512)(128)(4,1)}, pred[128]{0:T(512)(128)(4,1)S(1)}, u32[]{:S(2)}) copy-start(pred[128]{0:T(512)(128)(4,1)S(1)} %get-tuple-element.11) | copy-start | bytes 388
  8.4 138.2 %copy-start.8 = (s32[128]{0:T(128)}, s32[128]{0:T(128)S(1)}, u32[]{:S(2)}) copy-start(s32[128]{0:T(128)S(1)} %add_reduce_fusion) | copy-start | bytes 1540
  9.3 316.7 %all-gather.4.cloned.1.call-start = ((), (), s32[]{:S(2)}) async-start(), calls=%async_computation.1 | async-start | bytes 19464192 | tf_op jit(solution)/shard_map/all_gather | solution.py:52
  11.0 23.3 %copy-start.14 = (s32[2]{0:T(128)S(1)}, s32[2]{0:T(128)}, u32[]{:S(2)}) copy-start(s32[2]{0:T(128)} %constant.64) | copy-start | bytes 28
  11.0 23.3 %copy-start.13 = (s32[2]{0:T(128)S(1)}, s32[2]{0:T(128)}, u32[]{:S(2)}) copy-start(s32[2]{0:T(128)} %constant.67) | copy-start | bytes 28
  11.0 23.7 %copy-start.4 = (f32[128,32]{0,1:T(8,128)S(1)}, f32[128,32]{0,1:T(8,128)}, u32[]{:S(2)}) copy-start(f32[128,32]{0,1:T(8,128)} %param.15) | copy-start | bytes 49156
  133.6 11.6 %copy-start.12 = (u32[256]{0:T(256)S(1)}, u32[256]{0:T(256)}, u32[]{:S(2)}) copy-start(u32[256]{0:T(256)} %constant.74) | copy-start | bytes 3076
  133.6 13.0 %copy-start.11 = (s32[128]{0:T(128)S(1)}, s32[128]{0:T(128)}, u32[]{:S(2)}) copy-start(s32[128]{0:T(128)} %param.13) | copy-start | bytes 1540
  133.6 167.3 %all-to-all-start = ((bf16[128,32,500]{0,2,1:T(8,128)(2,1)}), bf16[128,32,500]{0,2,1:T(8,128)(2,1)}, u32[]{:S(2)}, u32[]{:S(2)}) async-start(bf16[128,32,500]{0,2,1:T(8,128)(2,1)} %copy.40), calls=%async_computation | async-start | bytes 8257536 | tf_op jit(solution)/shard_map/all_to_all | solution.py:48
  145.2 465.4 %all-reduce.6.cloned.1.call-start = ((), (), s32[]{:S(2)}) async-start(), calls=%async_computation.2 | async-start | bytes 1179648 | tf_op jit(solution)/shard_map/psum | solution.py:95
  326.0 18.5 %copy-start.10 = (f32[500]{0:T(512)S(1)}, f32[500]{0:T(512)}, u32[]{:S(2)}) copy-start(f32[500]{0:T(512)} %param.18) | copy-start | bytes 6004
  326.0 94.0 %copy-start.6 = (f32[2304]{0:T(1024)S(1)}, f32[2304]{0:T(1024)}, u32[]{:S(2)}) copy-start(f32[2304]{0:T(1024)} %param.19) | copy-start | bytes 27652
  345.1 196.0 %copy-start.7 = (f32[500]{0:T(512)}, f32[500]{0:T(512)S(1)}, u32[]{:S(2)}) copy-start(f32[500]{0:T(512)S(1)} %get-tuple-element.16) | copy-start | bytes 6004
  420.0 121.1 %copy-start.5 = (f32[2304]{0:T(1024)}, f32[2304]{0:T(1024)S(1)}, u32[]{:S(2)}) copy-start(f32[2304]{0:T(1024)S(1)} %multiply_add_fusion.1) | copy-start | bytes 27652
  506.1 29.4 %copy-start.3 = (bf16[24,2304]{1,0:T(8,128)(2,1)}, bf16[24,2304]{1,0:T(8,128)(2,1)S(1)}, u32[]{:S(2)}) copy-start(bf16[24,2304]{1,0:T(8,128)(2,1)S(1)} %fusion) | copy-start | bytes 331780
  506.1 19.9 %collective-permute-start.5 = (bf16[4,2304]{1,0:T(4,128)(2,1)S(1)}, bf16[4,2304]{1,0:T(4,128)(2,1)S(1)}, u32[]{:S(2)}, u32[]{:S(2)}) collective-permute-start(bf16[4,2304]{1,0:T(4,128)(2,1)S(1)} %slice.2), channel_id=1, source_target_pairs={{0,48},{8,56},{16,64},{24,72},{32,80},{40,88},{48,96},{56,104},{64... | collective-permute-start | bytes 55304
  508.0 27.4 %collective-permute-start = (bf16[24,2304]{1,0:T(8,128)(2,1)S(1)}, bf16[24,2304]{1,0:T(8,128)(2,1)S(1)}, u32[]{:S(2)}, u32[]{:S(2)}) collective-permute-start(bf16[24,2304]{1,0:T(8,128)(2,1)S(1)} %fusion), channel_id=1, source_target_pairs={{0,8},{8,16},{16,24},{24,32},{32,40},{40,48},{48,56},{56,64},{64,7... | collective-permute-start | bytes 331784
  510.2 25.3 %collective-permute-start.1 = (bf16[24,2304]{1,0:T(8,128)(2,1)S(1)}, bf16[24,2304]{1,0:T(8,128)(2,1)S(1)}, u32[]{:S(2)}, u32[]{:S(2)}) collective-permute-start(bf16[24,2304]{1,0:T(8,128)(2,1)S(1)} %fusion), channel_id=1, source_target_pairs={{0,16},{8,24},{16,32},{24,40},{32,48},{40,56},{48,64},{56,72},{64,... | collective-permute-start | bytes 331784
  514.9 20.6 %collective-permute-start.2 = (bf16[24,2304]{1,0:T(8,128)(2,1)S(1)}, bf16[24,2304]{1,0:T(8,128)(2,1)S(1)}, u32[]{:S(2)}, u32[]{:S(2)}) collective-permute-start(bf16[24,2304]{1,0:T(8,128)(2,1)S(1)} %fusion), channel_id=1, source_target_pairs={{0,24},{8,32},{16,40},{24,48},{32,56},{40,64},{48,72},{56,80},{64,... | collective-permute-start | bytes 331784
  518.1 17.3 %collective-permute-start.3 = (bf16[24,2304]{1,0:T(8,128)(2,1)S(1)}, bf16[24,2304]{1,0:T(8,128)(2,1)S(1)}, u32[]{:S(2)}, u32[]{:S(2)}) collective-permute-start(bf16[24,2304]{1,0:T(8,128)(2,1)S(1)} %fusion), channel_id=1, source_target_pairs={{0,32},{8,40},{16,48},{24,56},{32,64},{40,72},{48,80},{56,88},{64,... | collective-permute-start | bytes 331784
  526.0 11.1 %collective-permute-start.4 = (bf16[24,2304]{1,0:T(8,128)(2,1)S(1)}, bf16[24,2304]{1,0:T(8,128)(2,1)S(1)}, u32[]{:S(2)}, u32[]{:S(2)}) collective-permute-start(bf16[24,2304]{1,0:T(8,128)(2,1)S(1)} %fusion), channel_id=1, source_target_pairs={{0,40},{8,48},{16,56},{24,64},{32,72},{40,80},{48,88},{56,96},{64,... | collective-permute-start | bytes 331784
  537.1 75.3 %copy-start.1 = (bf16[128,2304]{1,0:T(8,128)(2,1)S(1)}, bf16[128,2304]{1,0:T(8,128)(2,1)}, u32[]{:S(2)}) copy-start(bf16[128,2304]{1,0:T(8,128)(2,1)} %param.12) | copy-start | bytes 1769476
Sparse Core Ops, SparseCore 0:
  11.2 81.9 all-gather.5
  95.7 230.1 all-gather.3
  541.2 69.2 all-reduce.5
where the time goes:
time: 620 us; the launch traced here: 619 us
  blocking collectives  326 us (53%)
  waiting for transfers between devices  85.8 us (14%)
  local copies, waits for them, and re-layouts  66.8 us (11%)
  other arithmetic  52.7 us (8%)
  starting transfers between devices  40.2 us (6%)
  matrix products  31.2 us (5%)
  between operations  16.1 us (3%)
    unnamed x2, blocking collectives  226 us
    psum x1, blocking collectives, body(): lax.psum((jnp.sum(squares, axis=0), jnp.sum(row_new)), ('dp', 'vocab'))  74.8 us
    psum x1, waiting for transfers between devices, body(): next_rows = lax.psum(spread.astype(jnp.bfloat16), 'vocab')  64.9 us
    unnamed x5, other arithmetic  31.9 us
    unnamed x6, starting transfers between devices  28.6 us
    all_to_all x3, local copies, waits for them, and re-layouts, body(): lax.all_to_all(slopes, 'dp', split_axis=1, concat_axis=0, tiled=True)  25.3 us
    gather x1, local copies, waits for them, and re-layouts, body(): mapped = vocab_map[target_ids] - vocab_index * shard_cols  23 us
    dot_general x1, matrix products, body(): jnp.einsum('tv,td->vd', owned_slopes, lax.all_gather(hidden, 'dp', axis=0...  18.5 us
  transfers between devices with their start and end apart: 10, of which 4 were waited for; matrix products, arithmetic and copies ran while one was open for 19% of the time, Pallas kernels for 0%

commit v1 on v0

--- a/solution.py
+++ b/solution.py
@@ -92,7 +92,9 @@
         tiled=True,
     )
     spread = jnp.einsum("st,sd->td", placing_half, slot_values, preferred_element_type=jnp.float32)
-    next_rows = lax.psum(spread.astype(jnp.bfloat16), "vocab")
+    own = spread.astype(jnp.bfloat16)
+    parts = lax.all_gather(own, "vocab")
+    next_rows = jnp.sum(parts, axis=0)
     return (direction.astype(jnp.bfloat16), row_new, col_new, next_rows)
 
 

time: 620 us -> 592 us (0.955)
  waiting for transfers between devices: 85.8 us -> 55.8 us
    psum x1 -> x0, waiting for transfers between devices: 64.9 us -> none  [body(): next_rows = lax.psum(spread.astype(jnp.bfloat16), 'vocab')]
    all_gather x0 -> x1, waiting for transfers between devices: none -> 35.1 us  [body(): parts = lax.all_gather(own, 'vocab')]
  transfers between devices with their start and end apart: 10 -> 10, of which waited for: 4 -> 4; matrix products, arithmetic and copies ran while one was open for 19% -> 20% of each run, Pallas kernels for 0% -> 0%
where the time goes in v1:
time: 592 us; the launch traced here: 590 us
  blocking collectives  326 us (55%)
  local copies, waits for them, and re-layouts  64.1 us (11%)
  other arithmetic  56.8 us (10%)
  waiting for transfers between devices  55.8 us (9%)
  starting transfers between devices  40.4 us (7%)
  matrix products  30.5 us (5%)
  between operations  16.1 us (3%)
    unnamed x2, blocking collectives  226 us
    psum x1, blocking collectives, body(): lax.psum((jnp.sum(squares, axis=0), jnp.sum(row_new)), ('dp', 'vocab'))  74.8 us
    all_gather x1, waiting for transfers between devices, body(): parts = lax.all_gather(own, 'vocab')  35.1 us
    unnamed x5, other arithmetic  31.9 us
    unnamed x6, starting transfers between devices  28.8 us
    all_to_all x3, local copies, waits for them, and re-layouts, body(): lax.all_to_all(slopes, 'dp', split_axis=1, concat_axis=0, tiled=True)  25.3 us
    gather x1, local copies, waits for them, and re-layouts, body(): mapped = vocab_map[target_ids] - vocab_index * shard_cols  23 us
    dot_general x1, matrix products, body(): jnp.einsum('tv,td->vd', owned_slopes, lax.all_gather(hidden, 'dp', axis=0...  18.5 us
  transfers between devices with their start and end apart: 10, of which 4 were waited for; matrix products, arithmetic and copies ran while one was open for 20% of the time, Pallas kernels for 0%

profile of v1, /device:TPU:8, one launch (start us, length us, event | category | flops | bytes accessed | tf_op | source)
XLA Modules:
  0.0 589.8 jit_solution(11917557533390439845)
XLA Ops:
  11.0 23.0 %gather_fusion = s32[4096]{0:T(1024)S(1)} fusion(s32[128256]{0:T(1024)S(1)} %copy-done.2, s32[4096]{0:T(1024)S(1)} %broadcast_clamp_fusion), kind=kCustom, calls=%fused_computation | custom fusion | bytes 49152 | tf_op jit(solution)/shard_map/gather | solution.py:37
  35.2 31.6 %scatter_custom_fusion = f32[2048000]{0:T(1024)} fusion(s32[4096]{0:T(1024)S(1)} %reshape.100, f32[4096]{0:T(1024)S(1)} %reshape.102, f32[]{:T(128)} %constant.22.clone.1), kind=kCustom, calls=%fused_computation.10 | custom fusion | flops 4096 | bytes 8192004
  66.8 9.1 %reshape.90 = f32[128,16000]{1,0:T(8,128)} reshape(f32[2048000]{0:T(1024)} %scatter_custom_fusion) | data formatting | bytes 16384000 | tf_op jit(solution)/shard_map/scatter-add | solution.py:45
  75.9 2.9 reduce_max.23
  78.8 13.1 %pmax.7 = f32[128]{0:T(128)S(1)} all-reduce(bf16[128]{0:T(256)(128)(2,1)S(1)} %reduce_max.23), channel_id=1, replica_groups=mesh['dp'=32,'vocab'=8] {'vocab'}, use_global_device_ids=true, to_apply=%region_1.0 | all-reduce | flops 128 | bytes 768 | tf_op jit(solution)/shard_map/pmax | solution.py:31
  91.9 3.7 fusion.1
  95.5 12.4 %psum.21 = f32[128]{0:T(128)S(1)} all-reduce(f32[128]{0:T(128)S(1)} %fusion.1), channel_id=1, replica_groups=mesh['dp'=32,'vocab'=8] {'vocab'}, use_global_device_ids=true, to_apply=%region_3.0 | all-reduce | flops 128 | bytes 1024 | tf_op jit(solution)/shard_map/psum | solution.py:32
  108.0 6.9 %subtract_convert_fusion = bf16[128,16000]{1,0:T(8,128)(2,1)} fusion(f32[128,16000]{1,0:T(8,128)} %reshape.90, bf16[128,16000]{1,0:T(8,128)(2,1)} %param.10, f32[128]{0:T(128)S(1)} %psum.21, f32[128]{0:T(128)S(1)} %pmax.7), kind=kLoop, calls=%fused_computation.2 | loop fusion | flops 10240000 | bytes 16385024 | tf_op jit(solution)/shard_map/convert_element_type | solution.py:47
  114.9 10.9 %reshape.127 = bf16[128,32,500]{2,1,0:T(8,128)(2,1)} reshape(bf16[128,16000]{1,0:T(8,128)(2,1)} %subtract_convert_fusion) | data formatting | bytes 8192000 | tf_op jit(solution)/shard_map/all_to_all | solution.py:48
  125.7 7.9 %copy.40 = bf16[128,32,500]{0,2,1:T(8,128)(2,1)} copy(bf16[128,32,500]{2,1,0:T(8,128)(2,1)} %reshape.127) | data formatting | bytes 8192000 | tf_op jit(solution)/shard_map/all_to_all | solution.py:48
  133.6 11.5 %all-to-all-start = ((bf16[128,32,500]{0,2,1:T(8,128)(2,1)}), bf16[128,32,500]{0,2,1:T(8,128)(2,1)}, u32[]{:S(2)}, u32[]{:S(2)}) async-start(bf16[128,32,500]{0,2,1:T(8,128)(2,1)} %copy.40), calls=%async_computation | async-start | bytes 8257536 | tf_op jit(solution)/shard_map/all_to_all | solution.py:48
  146.8 146.2 %all-reduce = s32[640]{0:T(1024)S(1)} all-reduce(s32[640]{0:T(1024)S(1)} %select_dynamic-update-slice_fusion), channel_id=1, replica_groups=mesh['dp'=32,'vocab'=8] {'dp'}, use_global_device_ids=true, to_apply=%add | all-reduce | flops 640 | bytes 5120
  293.0 3.8 reshape.124
  296.8 4.1 fusion.8
  301.0 6.6 %copy.38 = bf16[32,128,500]{2,1,0:T(8,128)(2,1)} copy(bf16[32,128,500]{1,2,0:T(8,128)(2,1)} %bitcast) | data formatting | bytes 8192000 | tf_op jit(solution)/shard_map/all_to_all | solution.py:48
  307.5 18.4 %all-gather.6.cloned.1.call-done = bf16[4096,2304]{1,0:T(8,128)(2,1)} async-done(((bf16[128,2304]{1,0:T(8,128)(2,1)}), bf16[4096,2304]{1,0:T(8,128)(2,1)}) %all-gather.6.cloned.1.call-update) | async-done | bytes 18874384 | tf_op jit(solution)/shard_map/all_gather | solution.py:52
  326.0 18.5 %fusion.4 = (f32[2304]{0:T(1024)S(1)}, f32[500]{0:T(512)S(1)}, f32[500,2304]{1,0:T(8,128)}) fusion(f32[500,2304]{1,0:T(8,128)} %fusion.8, bf16[4096,500]{1,0:T(8,128)(2,1)} %bitcast.16, bf16[4096,2304]{1,0:T(8,128)(2,1)} %all-gather.6.cloned.1.call-done), kind=kOutput, calls=%fused_computation.12 | convolution fusion | flops 9442941952 | bytes 32197584 | tf_op jit(solution)/shard_map/tv,td->vd/dot_general | solution.py:49
  345.1 74.8 %all-reduce.3 = (f32[]{:T(128)}, f32[2304]{0:T(1024)S(1)}) all-reduce(f32[]{:T(128)} %get-tuple-element.8, f32[2304]{0:T(1024)S(1)} %get-tuple-element.4), channel_id=1, replica_groups=mesh['dp'=32,'vocab'=8] {'dp','vocab'}, use_global_device_ids=true, to_apply=%region_14.15 | all-reduce | flops 2305 | bytes 18440 | tf_op jit(solution)/shard_map/psum | solution.py:78
  420.7 5.8 convolution_convert_fusion
  426.4 79.7 %fusion = bf16[24,2304]{1,0:T(8,128)(2,1)S(1)} fusion(bf16[640,2304]{1,0:T(8,128)(2,1)S(1)} %convolution_convert_fusion), kind=kCustom, calls=%all-reduce-scatter | all-reduce-scatter fusion | flops 1769473 | bytes 3060736
  506.1 1.9 collective-permute-start.5
  508.0 2.1 collective-permute-start
  510.2 4.7 collective-permute-start.1
  514.9 3.3 collective-permute-start.2
  518.1 7.8 %collective-permute-start.3 = (bf16[24,2304]{1,0:T(8,128)(2,1)S(1)}, bf16[24,2304]{1,0:T(8,128)(2,1)S(1)}, u32[]{:S(2)}, u32[]{:S(2)}) collective-permute-start(bf16[24,2304]{1,0:T(8,128)(2,1)S(1)} %fusion), channel_id=1, source_target_pairs={{0,32},{8,40},{16,48},{24,56},{32,64},{40,72},{48,80},{56,88},{64,... | collective-permute-start | bytes 331784
  526.0 9.0 %collective-permute-start.4 = (bf16[24,2304]{1,0:T(8,128)(2,1)S(1)}, bf16[24,2304]{1,0:T(8,128)(2,1)S(1)}, u32[]{:S(2)}, u32[]{:S(2)}) collective-permute-start(bf16[24,2304]{1,0:T(8,128)(2,1)S(1)} %fusion), channel_id=1, source_target_pairs={{0,40},{8,48},{16,56},{24,64},{32,72},{40,80},{48,88},{56,96},{64,... | collective-permute-start | bytes 331784
  535.7 1.4 collective-permute-done.4
  537.1 1.3 concatenate.4
  538.4 1.2 convolution_convert_fusion.1
  539.7 4.5 fusion.23
  544.2 35.1 %all-gather.8.cloned.1.call-done = bf16[1024,2304]{1,0:T(8,128)(2,1)} async-done(((bf16[128,2304]{1,0:T(8,128)(2,1)}), bf16[1024,2304]{1,0:T(8,128)(2,1)}) %all-gather.8.cloned.1.call-update) | async-done | bytes 4718608 | tf_op jit(solution)/shard_map/all_gather | solution.py:96
  579.3 4.0 reduce_sum.72
  (80 shorter events, 6.6 us)
Async XLA Ops:
  7.2 1.2 copy-start
  7.2 3.8 copy-start.2
  7.2 285.8 %all-gather.10.cloned.1.call-start = ((), (), s32[]{:S(2)}) async-start(), calls=%async_computation.3 | async-start | bytes 3649536 | tf_op jit(solution)/shard_map/all_gather | solution.py:70
  8.0 138.6 %copy-start.9 = (pred[128]{0:T(512)(128)(4,1)}, pred[128]{0:T(512)(128)(4,1)S(1)}, u32[]{:S(2)}) copy-start(pred[128]{0:T(512)(128)(4,1)S(1)} %get-tuple-element.11) | copy-start | bytes 388
  8.4 138.2 %copy-start.7 = (s32[128]{0:T(128)}, s32[128]{0:T(128)S(1)}, u32[]{:S(2)}) copy-start(s32[128]{0:T(128)S(1)} %add_reduce_fusion) | copy-start | bytes 1540
  9.3 316.7 %all-gather.6.cloned.1.call-start = ((), (), s32[]{:S(2)}) async-start(), calls=%async_computation.1 | async-start | bytes 19464192 | tf_op jit(solution)/shard_map/all_gather | solution.py:52
  11.0 23.3 %copy-start.15 = (s32[2]{0:T(128)S(1)}, s32[2]{0:T(128)}, u32[]{:S(2)}) copy-start(s32[2]{0:T(128)} %constant.66) | copy-start | bytes 28
  11.0 23.3 %copy-start.14 = (s32[2]{0:T(128)S(1)}, s32[2]{0:T(128)}, u32[]{:S(2)}) copy-start(s32[2]{0:T(128)} %constant.69) | copy-start | bytes 28
  11.0 23.7 %copy-start.3 = (f32[128,32]{0,1:T(8,128)S(1)}, f32[128,32]{0,1:T(8,128)}, u32[]{:S(2)}) copy-start(f32[128,32]{0,1:T(8,128)} %param.15) | copy-start | bytes 49156
  133.6 11.6 %copy-start.13 = (u32[256]{0:T(256)S(1)}, u32[256]{0:T(256)}, u32[]{:S(2)}) copy-start(u32[256]{0:T(256)} %constant.76) | copy-start | bytes 3076
  133.6 13.0 %copy-start.12 = (s32[128]{0:T(128)S(1)}, s32[128]{0:T(128)}, u32[]{:S(2)}) copy-start(s32[128]{0:T(128)} %param.13) | copy-start | bytes 1540
  133.6 167.3 %all-to-all-start = ((bf16[128,32,500]{0,2,1:T(8,128)(2,1)}), bf16[128,32,500]{0,2,1:T(8,128)(2,1)}, u32[]{:S(2)}, u32[]{:S(2)}) async-start(bf16[128,32,500]{0,2,1:T(8,128)(2,1)} %copy.40), calls=%async_computation | async-start | bytes 8257536 | tf_op jit(solution)/shard_map/all_to_all | solution.py:48
  145.2 434.2 %all-gather.8.cloned.1.call-start = ((), (), s32[]{:S(2)}) async-start(), calls=%async_computation.2 | async-start | bytes 5308416 | tf_op jit(solution)/shard_map/all_gather | solution.py:96
  326.0 18.5 %copy-start.11 = (f32[500]{0:T(512)S(1)}, f32[500]{0:T(512)}, u32[]{:S(2)}) copy-start(f32[500]{0:T(512)} %param.18) | copy-start | bytes 6004
  326.0 94.0 %copy-start.5 = (f32[2304]{0:T(1024)S(1)}, f32[2304]{0:T(1024)}, u32[]{:S(2)}) copy-start(f32[2304]{0:T(1024)} %param.19) | copy-start | bytes 27652
  345.1 194.5 %copy-start.6 = (f32[500]{0:T(512)}, f32[500]{0:T(512)S(1)}, u32[]{:S(2)}) copy-start(f32[500]{0:T(512)S(1)} %get-tuple-element.9) | copy-start | bytes 6004
  420.0 119.7 %copy-start.4 = (f32[2304]{0:T(1024)}, f32[2304]{0:T(1024)S(1)}, u32[]{:S(2)}) copy-start(f32[2304]{0:T(1024)S(1)} %multiply_add_fusion.1) | copy-start | bytes 27652
  420.6 117.8 %copy-start.8 = (s32[128]{0:T(128)S(1)}, s32[128]{0:T(128)}, u32[]{:S(2)}) copy-start(s32[128]{0:T(128)} %copy-done.7) | copy-start | bytes 1540
  420.6 117.8 %copy-start.10 = (pred[128]{0:T(512)(128)(4,1)S(1)}, pred[128]{0:T(512)(128)(4,1)}, u32[]{:S(2)}) copy-start(pred[128]{0:T(512)(128)(4,1)} %copy-done.9) | copy-start | bytes 388
  506.1 19.9 %collective-permute-start.5 = (bf16[4,2304]{1,0:T(4,128)(2,1)S(1)}, bf16[4,2304]{1,0:T(4,128)(2,1)S(1)}, u32[]{:S(2)}, u32[]{:S(2)}) collective-permute-start(bf16[4,2304]{1,0:T(4,128)(2,1)S(1)} %slice.2), channel_id=1, source_target_pairs={{0,48},{8,56},{16,64},{24,72},{32,80},{40,88},{48,96},{56,104},{64... | collective-permute-start | bytes 55304
  508.0 27.6 %collective-permute-start = (bf16[24,2304]{1,0:T(8,128)(2,1)S(1)}, bf16[24,2304]{1,0:T(8,128)(2,1)S(1)}, u32[]{:S(2)}, u32[]{:S(2)}) collective-permute-start(bf16[24,2304]{1,0:T(8,128)(2,1)S(1)} %fusion), channel_id=1, source_target_pairs={{0,8},{8,16},{16,24},{24,32},{32,40},{40,48},{48,56},{56,64},{64,7... | collective-permute-start | bytes 331784
  510.2 25.5 %collective-permute-start.1 = (bf16[24,2304]{1,0:T(8,128)(2,1)S(1)}, bf16[24,2304]{1,0:T(8,128)(2,1)S(1)}, u32[]{:S(2)}, u32[]{:S(2)}) collective-permute-start(bf16[24,2304]{1,0:T(8,128)(2,1)S(1)} %fusion), channel_id=1, source_target_pairs={{0,16},{8,24},{16,32},{24,40},{32,48},{40,56},{48,64},{56,72},{64,... | collective-permute-start | bytes 331784
  514.9 20.9 %collective-permute-start.2 = (bf16[24,2304]{1,0:T(8,128)(2,1)S(1)}, bf16[24,2304]{1,0:T(8,128)(2,1)S(1)}, u32[]{:S(2)}, u32[]{:S(2)}) collective-permute-start(bf16[24,2304]{1,0:T(8,128)(2,1)S(1)} %fusion), channel_id=1, source_target_pairs={{0,24},{8,32},{16,40},{24,48},{32,56},{40,64},{48,72},{56,80},{64,... | collective-permute-start | bytes 331784
  518.1 17.6 %collective-permute-start.3 = (bf16[24,2304]{1,0:T(8,128)(2,1)S(1)}, bf16[24,2304]{1,0:T(8,128)(2,1)S(1)}, u32[]{:S(2)}, u32[]{:S(2)}) collective-permute-start(bf16[24,2304]{1,0:T(8,128)(2,1)S(1)} %fusion), channel_id=1, source_target_pairs={{0,32},{8,40},{16,48},{24,56},{32,64},{40,72},{48,80},{56,88},{64,... | collective-permute-start | bytes 331784
  526.0 11.1 %collective-permute-start.4 = (bf16[24,2304]{1,0:T(8,128)(2,1)S(1)}, bf16[24,2304]{1,0:T(8,128)(2,1)S(1)}, u32[]{:S(2)}, u32[]{:S(2)}) collective-permute-start(bf16[24,2304]{1,0:T(8,128)(2,1)S(1)} %fusion), channel_id=1, source_target_pairs={{0,40},{8,48},{16,56},{24,64},{32,72},{40,80},{48,88},{56,96},{64,... | collective-permute-start | bytes 331784
  539.6 43.6 %copy-start.1 = (bf16[128,2304]{1,0:T(8,128)(2,1)S(1)}, bf16[128,2304]{1,0:T(8,128)(2,1)}, u32[]{:S(2)}) copy-start(bf16[128,2304]{1,0:T(8,128)(2,1)} %param.12) | copy-start | bytes 1769476
Sparse Core Ops, SparseCore 0:
  11.2 81.9 all-gather.9
  95.7 230.1 all-gather.5
  539.7 39.5 all-gather.7
